TPU v7x, 32 devices: a whole 2x2x4 slice. The times are simulated.
32 devices in a mesh: req: 4 (over y, core), ad: 8 (over z, x).
Axes of the slice: x: 2, y: 2, z: 4, core: 2. Of those that a mesh axis runs over, the one named last changes fastest.
Arguments:
- residual: bfloat16 [256, 32, 1152], P(('req', 'ad')), may hold values from -16 to 16
- lengths: int32 [256], P(('req', 'ad')), may hold values from 1 to 32, 7168 in all
- adapter_ids: int32 [256], P(('req', 'ad')), may hold values from 0 to 31, as said below
- ffn_gain: float32 [1152], replicated, may hold values from 0.5 to 1.5
- w_gate_up: bfloat16 [2, 1152, 3072], replicated, may hold values from -0.1875 to 0.1875
- w_down: bfloat16 [3072, 1152], replicated, may hold values from -0.109375 to 0.109375
- adapter_input_first: bfloat16 [32, 32, 1152], P('ad'), may hold values from -0.1875 to 0.1875
- ad_out_b: bfloat16 [32, 2, 16, 3072], P('ad'), may hold values from -1.5 to 1.5
- ad_down_a: bfloat16 [32, 16, 3072], P('ad'), may hold values from -0.109375 to 0.109375
- adapter_down_second: bfloat16 [32, 16, 1152], P('ad'), may hold values from -1.5 to 1.5
- final_gain: float32 [1152], replicated, may hold values from 0.5 to 1.5
- head_weight: bfloat16 [1152, 32000], P(None, ('req', 'ad')), may hold values from -3 to 3
Outputs:
- layer_out: bfloat16 [256, 32, 1152], P(('req', 'ad'))
- log_probs: float32 [256, 32000], P(None, ('req', 'ad'))
Inputs may be any that keep to these rules, and one draw needn't show every extreme that they name: `adapter_ids`: the 8 requests of one device (aligned blocks of 8 requests in order) use adapters whose indices divided by 4 are all different.
All inputs are finite; a program needn't handle non-finite values. No bound on the sum of `lengths` on one device may be relied on, other than what follows from the above.
Results may differ from a plain program's by a relative error of at most 0.0076.
Values may be sent and summed in bfloat16 or wider, within the bound.
A program may use at most 128 MiB of HBM per device.

v0:
```python
import jax
import jax.numpy as jnp
from jax import lax
from jax.sharding import PartitionSpec as P

epsilon = 1e-05


def rms_scale(values, gain):
    mean_sq = jnp.mean(values * values, axis=-1, keepdims=True)
    return values * lax.rsqrt(mean_sq + epsilon) * gain


def picks_of(slot_ids, per_dev):
    return (slot_ids[..., None] == jnp.arange(per_dev, dtype=jnp.int32)).astype(jnp.float32)


def adapter_gate_up(row_block, picks, in_a, out_b):
    lowered = jnp.einsum("isd,akd->isak", row_block, in_a, preferred_element_type=jnp.float32)
    input_lowrank_state = jnp.sum(lowered * picks[..., None], axis=2).astype(jnp.bfloat16)
    spread = input_lowrank_state[:, :, None, :] * picks[..., None].astype(jnp.bfloat16)
    rank = out_b.shape[2]
    spread = spread.reshape(spread.shape[0], spread.shape[1], spread.shape[2], 2, rank)
    return jnp.einsum("isajr,ajrf->isjf", spread, out_b, preferred_element_type=jnp.float32).astype(
        jnp.bfloat16
    )


def adapter_down(hidden_block, picks, down_a, down_b):
    lowered = jnp.einsum("isf,akf->isak", hidden_block, down_a, preferred_element_type=jnp.float32)
    down_lowrank_state = jnp.sum(lowered * picks[..., None], axis=2).astype(jnp.bfloat16)
    spread = down_lowrank_state[:, :, None, :] * picks[..., None].astype(jnp.bfloat16)
    return jnp.einsum("isak,akd->isd", spread, down_b, preferred_element_type=jnp.float32).astype(
        jnp.bfloat16
    )


def base_gate_up(normalized_rows, w_gate_up):
    lead = normalized_rows.shape[:-1]
    flat = normalized_rows.reshape(-1, normalized_rows.shape[-1])
    gate = jnp.dot(flat, w_gate_up[0], preferred_element_type=jnp.float32)
    up_part = jnp.dot(flat, w_gate_up[1], preferred_element_type=jnp.float32)
    return (gate.reshape(lead + (gate.shape[-1],)), up_part.reshape(lead + (up_part.shape[-1],)))


def base_down(hidden, w_down):
    lead = hidden.shape[:-1]
    result = jnp.dot(
        hidden.reshape(-1, hidden.shape[-1]), w_down, preferred_element_type=jnp.float32
    )
    return result.reshape(lead + (result.shape[-1],))


def local(
    residual,
    lengths,
    adapter_ids,
    ffn_gain,
    w_gate_up,
    w_down,
    adapter_input_first,
    ad_out_b,
    ad_down_a,
    adapter_down_second,
    final_gain,
    head_weight,
):
    req_dev, seq_len, width = residual.shape
    groups = lax.axis_size("ad")
    per_dev = adapter_input_first.shape[0]
    positions = jnp.arange(seq_len, dtype=jnp.int32)
    valid = positions[None, :] < lengths[:, None]
    stream = residual.astype(jnp.float32)
    normalized_rows = rms_scale(stream, ffn_gain).astype(jnp.bfloat16)
    kept = jnp.where(valid[..., None], normalized_rows, jnp.zeros_like(normalized_rows))
    holder = adapter_ids // per_dev
    local_id = adapter_ids % per_dev
    placing = jnp.arange(groups, dtype=jnp.int32)[:, None] == holder[None, :]
    place_bf = placing.astype(jnp.bfloat16)
    slot_ids = jnp.sum(placing.astype(jnp.int32) * local_id[None, :], axis=1)
    slot_rows = jnp.broadcast_to(slot_ids[:, None], (groups, seq_len))

    def place(values):
        return jnp.einsum(
            "hr,rsf->hsf", place_bf, values, preferred_element_type=jnp.float32
        ).astype(jnp.bfloat16)

    def unplace(returned):
        return jnp.einsum("hr,hsf->rsf", place_bf, returned, preferred_element_type=jnp.float32)

    row_block = lax.all_to_all(place(kept), "ad", split_axis=0, concat_axis=0, tiled=True)
    row_ids = lax.all_to_all(slot_rows, "ad", split_axis=0, concat_axis=0, tiled=True)
    delta = adapter_gate_up(row_block, picks_of(row_ids, per_dev), adapter_input_first, ad_out_b)
    delta = delta.reshape(delta.shape[0], delta.shape[1], -1)
    returned_gu = lax.all_to_all(delta, "ad", split_axis=0, concat_axis=0, tiled=True)
    gate, up_part = base_gate_up(normalized_rows, w_gate_up)
    hidden_units = gate.shape[-1]
    delta_gu = unplace(returned_gu)
    hidden = (
        jax.nn.silu(gate + delta_gu[..., :hidden_units]) * (up_part + delta_gu[..., hidden_units:])
    ).astype(jnp.bfloat16)
    hidden_kept = jnp.where(valid[..., None], hidden, jnp.zeros_like(hidden))
    hidden_block = lax.all_to_all(place(hidden_kept), "ad", split_axis=0, concat_axis=0, tiled=True)
    row_ids = lax.all_to_all(slot_rows, "ad", split_axis=0, concat_axis=0, tiled=True)
    delta = adapter_down(hidden_block, picks_of(row_ids, per_dev), ad_down_a, adapter_down_second)
    returned_down = lax.all_to_all(delta, "ad", split_axis=0, concat_axis=0, tiled=True)
    mixed = stream + base_down(hidden, w_down) + unplace(returned_down)
    layer_out = jnp.where(valid[..., None], mixed, jnp.zeros_like(mixed)).astype(jnp.bfloat16)
    last_index = (lengths - 1)[:, None, None]
    last_row = jnp.take_along_axis(layer_out, last_index, axis=1)[:, 0, :].astype(jnp.float32)
    final = rms_scale(last_row, final_gain).astype(jnp.bfloat16)
    logits = jnp.dot(
        lax.all_gather(final, ("req", "ad"), axis=0, tiled=True),
        head_weight,
        preferred_element_type=jnp.float32,
    )
    local_max = jnp.max(logits, axis=1)
    highest = lax.pmax(local_max, ("req", "ad"))
    total = lax.psum(jnp.sum(jnp.exp(logits - highest[:, None]), axis=1), ("req", "ad"))
    log_probs = logits - highest[:, None] - jnp.log(total)[:, None]
    return (layer_out, log_probs)


def solution(mesh):
    in_specs = (
        P(("req", "ad"), None, None),
        P(("req", "ad")),
        P(("req", "ad")),
        P(),
        P(),
        P(),
        P("ad", None, None),
        P("ad", None, None, None),
        P("ad", None, None),
        P("ad", None, None),
        P(),
        P(None, ("req", "ad")),
    )
    out_specs = (P(("req", "ad"), None, None), P(None, ("req", "ad")))
    return jax.shard_map(local, mesh=mesh, in_specs=in_specs, out_specs=out_specs, check_vma=False)
```

profile of v0, /device:TPU:0, one launch (start us, length us, event | category | flops | bytes accessed | tf_op | source)
XLA Modules:
  0.0 355.6 jit_solution(7166750114568926179)
XLA Ops:
  2.2 7.3 %all-to-all-start.1 = ((s32[8,1,32]{2,1,0:T(1,128)}), s32[8,1,32]{2,1,0:T(1,128)S(1)}, u32[]{:S(2)}, u32[]{:S(2)}) async-start(s32[8,1,32]{2,1,0:T(1,128)} %broadcast_in_dim.35), calls=%async_computation.1 | async-start | bytes 8192 | tf_op jit(solution)/shard_map/all_to_all | solution.py:92
  9.5 1.2 fusion.40
  11.5 1.4 broadcast_select_fusion.1
  14.2 1.7 all-to-all-done.1
  15.9 4.3 %all-to-all-start = ((bf16[8,32,1152]{2,1,0:T(8,128)(2,1)}), bf16[8,32,1152]{2,1,0:T(8,128)(2,1)}, u32[]{:S(2)}, u32[]{:S(2)}) async-start(bf16[8,32,1152]{2,1,0:T(8,128)(2,1)} %copy.48), calls=%async_computation | async-start | bytes 1179648 | tf_op jit(solution)/shard_map/all_to_all | solution.py:91
  20.2 15.5 %all-to-all-done = bf16[8,32,1152]{2,1,0:T(8,128)(2,1)} async-done(((bf16[8,32,1152]{2,1,0:T(8,128)(2,1)}), bf16[8,32,1152]{2,1,0:T(8,128)(2,1)}, u32[]{:S(2)}, u32[]{:S(2)}) %all-to-all-start) | async-done | bytes 589856 | tf_op jit(solution)/shard_map/all_to_all | solution.py:91
  35.7 1.6 fusion.39
  38.7 74.3 %all_to_all.27 = bf16[8,32,6144]{2,1,0:T(8,128)(2,1)S(1)} all-to-all(bf16[8,32,6144]{2,1,0:T(8,128)(2,1)S(1)} %bitcast.85), channel_id=1, replica_groups=mesh['req'=4,'ad'=8] {'ad'}, dimensions={0} | all-to-all | bytes 6291456 | tf_op jit(solution)/shard_map/all_to_all | solution.py:95
  113.0 3.5 fusion.21
  118.1 3.9 %fusion.9 = f32[8,32,3072]{2,1,0:T(8,128)S(1)} fusion(bf16[2,1152,3072]{2,1,0:T(8,128)(2,1)S(1)} %bitcast.89, f32[8,32,3072]{2,0,1:T(8,128)S(1)} %get-tuple-element.2, bf16[8,32,1152]{2,1,0:T(8,128)(2,1)S(1)} %copy-done.1, f32[1152]{0:T(1024)S(1)} %copy-done.4, f32[8,32]{1,0:T(8,128)S(1)} %add_rsqrt_fusion), kind=kOutput, calls=%fused_computation.11 | convolution fusion | flops 1813905408 | bytes 13971456 | tf_op jit(solution)/shard_map/dot_general | solution.py:41
  122.1 5.1 %broadcast_select_fusion = (bf16[8,32,3072]{2,1,0:T(8,128)(2,1)S(1)}, bf16[8,32,3072]{2,1,0:T(8,128)(2,1)}) fusion(pred[8,32]{1,0:T(8,128)(4,1)S(1)} %iota_compare_fusion.2, f32[8,32,3072]{2,0,1:T(8,128)S(1)} %get-tuple-element.3, bf16[2,1152,3072]{2,1,0:T(8,128)(2,1)S(1)} %bitcast.89, bf16[8,32,1152]{2,1,0:T(8,128)(2,1)S(1)} %copy-done.1, ...), kind=kOutput, calls=%fused_computation.30 | convolution fusion | flops 1819410432 | bytes 17118208 | tf_op jit(solution)/shard_map/dot_general | solution.py:42
  127.2 1.2 convolution_convert_fusion
  128.4 2.0 copy.58
  130.4 4.5 %all-to-all-start.3 = ((bf16[8,32,3072]{2,1,0:T(8,128)(2,1)}), bf16[8,32,3072]{2,1,0:T(8,128)(2,1)}, u32[]{:S(2)}, u32[]{:S(2)}) async-start(bf16[8,32,3072]{2,1,0:T(8,128)(2,1)} %copy.58), calls=%async_computation.3 | async-start | bytes 3145728 | tf_op jit(solution)/shard_map/all_to_all | solution.py:103
  135.8 35.1 %all-to-all-done.3 = bf16[8,32,3072]{2,1,0:T(8,128)(2,1)} async-done(((bf16[8,32,3072]{2,1,0:T(8,128)(2,1)}), bf16[8,32,3072]{2,1,0:T(8,128)(2,1)}, u32[]{:S(2)}, u32[]{:S(2)}) %all-to-all-start.3) | async-done | bytes 1572896 | tf_op jit(solution)/shard_map/all_to_all | solution.py:103
  170.8 3.6 %fusion.36 = f32[8,32,4,16]{1,3,2,0:T(8,128)} fusion(bf16[8,32,3072]{2,1,0:T(8,128)(2,1)} %all-to-all-done.3, bf16[4,16,3072]{2,1,0:T(8,128)(2,1)} %param.20), kind=kOutput, calls=%fused_computation.27 | convolution fusion | flops 100663296 | bytes 2031616 | tf_op jit(solution)/shard_map/isf,akf->isak/dot_general | solution.py:30
  174.4 1.4 copy.73
  176.3 1.5 fusion.32
  178.7 3.6 %all-to-all-start.4 = ((bf16[8,32,1152]{2,1,0:T(8,128)(2,1)}), bf16[8,32,1152]{2,1,0:T(8,128)(2,1)S(1)}, u32[]{:S(2)}, u32[]{:S(2)}) async-start(bf16[8,32,1152]{2,1,0:T(8,128)(2,1)} %copy.64), calls=%async_computation.4 | async-start | bytes 1179648 | tf_op jit(solution)/shard_map/all_to_all | solution.py:106
  182.3 16.0 %all-to-all-done.4 = bf16[8,32,1152]{2,1,0:T(8,128)(2,1)S(1)} async-done(((bf16[8,32,1152]{2,1,0:T(8,128)(2,1)}), bf16[8,32,1152]{2,1,0:T(8,128)(2,1)S(1)}, u32[]{:S(2)}, u32[]{:S(2)}) %all-to-all-start.4) | async-done | bytes 589856 | tf_op jit(solution)/shard_map/all_to_all | solution.py:106
  198.7 5.9 %fusion.33 = bf16[8,32,1152]{2,1,0:T(8,128)(2,1)S(1)} fusion(bf16[8,32,3072]{2,1,0:T(8,128)(2,1)} %get-tuple-element.9, bf16[3072,1152]{1,0:T(8,128)(2,1)} %param.17, bf16[8,32,1152]{2,1,0:T(8,128)(2,1)S(1)} %copy-done.1, f32[8,32,1152]{2,0,1:T(8,128)S(1)} %fusion.45, pred[8,32]{1,0:T(8,128)(4,1)S(1)} %copy-done.7), kind=kOutput, calls=%fused_computation.23 | convolution fusion | flops 1813413888 | bytes 11010304 | tf_op jit(solution)/shard_map/dot_general | solution.py:48
  205.6 69.7 %all_gather.3 = bf16[256,1152]{1,0:T(8,128)(2,1)S(1)} all-gather(bf16[8,1152]{1,0:T(8,128)(2,1)S(1)} %fusion.61), channel_id=1, replica_groups=mesh['req'=4,'ad'=8] {'req','ad'}, dimensions={0}, use_global_device_ids=true | all-gather | bytes 608256 | tf_op jit(solution)/shard_map/all_gather | solution.py:113
  276.2 36.9 %pmax.7 = f32[256]{0:T(256)S(1)} all-reduce(f32[256]{0:T(256)S(1)} %get-tuple-element.10), channel_id=1, replica_groups=mesh['req'=4,'ad'=8] {'req','ad'}, use_global_device_ids=true, to_apply=%region_6.7 | all-reduce | flops 256 | bytes 2048 | tf_op jit(solution)/shard_map/pmax | solution.py:118
  313.3 41.3 %psum.7 = f32[256]{0:T(256)S(1)} all-reduce(f32[256]{0:T(256)S(1)} %exponential_reduce_fusion), channel_id=1, replica_groups=mesh['req'=4,'ad'=8] {'req','ad'}, use_global_device_ids=true, to_apply=%region_8.9 | all-reduce | flops 256 | bytes 2048 | tf_op jit(solution)/shard_map/psum | solution.py:119
  (61 shorter events, 12.2 us)
Async XLA Ops:
  0.6 274.6 %copy-start = (bf16[1152,1000]{0,1:T(8,128)(2,1)S(1)}, bf16[1152,1000]{0,1:T(8,128)(2,1)}, u32[]{:S(2)}) copy-start(bf16[1152,1000]{0,1:T(8,128)(2,1)} %param.23) | copy-start | bytes 6912004
  2.2 13.6 %all-to-all-start.1 = ((s32[8,1,32]{2,1,0:T(1,128)}), s32[8,1,32]{2,1,0:T(1,128)S(1)}, u32[]{:S(2)}, u32[]{:S(2)}) async-start(s32[8,1,32]{2,1,0:T(1,128)} %broadcast_in_dim.35), calls=%async_computation.1 | async-start | bytes 8192 | tf_op jit(solution)/shard_map/all_to_all | solution.py:92
  11.5 110.6 %copy-start.6 = (pred[8,32]{1,0:T(8,128)(4,1)}, pred[8,32]{1,0:T(8,128)(4,1)S(1)}, u32[]{:S(2)}) copy-start(pred[8,32]{1,0:T(8,128)(4,1)S(1)} %iota_compare_fusion.2) | copy-start | bytes 772
  11.5 24.2 %copy-start.8 = (bf16[4,32,1152]{2,1,0:T(8,128)(2,1)S(1)}, bf16[4,32,1152]{2,1,0:T(8,128)(2,1)}, u32[]{:S(2)}) copy-start(bf16[4,32,1152]{2,1,0:T(8,128)(2,1)} %param.18) | copy-start | bytes 884740
  13.3 24.1 %copy-start.2 = (bf16[4,2,16,3072]{3,2,1,0:T(8,128)(2,1)S(1)}, bf16[4,2,16,3072]{3,2,1,0:T(8,128)(2,1)}, u32[]{:S(2)}) copy-start(bf16[4,2,16,3072]{3,2,1,0:T(8,128)(2,1)} %param.19) | copy-start | bytes 2359300
  15.9 19.8 %all-to-all-start = ((bf16[8,32,1152]{2,1,0:T(8,128)(2,1)}), bf16[8,32,1152]{2,1,0:T(8,128)(2,1)}, u32[]{:S(2)}, u32[]{:S(2)}) async-start(bf16[8,32,1152]{2,1,0:T(8,128)(2,1)} %copy.48), calls=%async_computation | async-start | bytes 1179648 | tf_op jit(solution)/shard_map/all_to_all | solution.py:91
  38.4 78.9 %slice-start = ((s8[14155776]{0:T(1024)(128)(4,1)}), s8[4194304]{0:T(1024)(128)(4,1)S(1)}, s32[]{:S(2)}) async-start(s8[14155776]{0:T(1024)(128)(4,1)} %bitcast.88), calls=%async_computation.5 | async-start | bytes 8388608
  38.7 78.6 %slice-start.1 = ((s8[14155776]{0:T(1024)(128)(4,1)}), s8[4194304]{0:T(1024)(128)(4,1)S(1)}, s32[]{:S(2)}) async-start(s8[14155776]{0:T(1024)(128)(4,1)} %bitcast.88), calls=%async_computation.6 | async-start | bytes 8388608
  113.0 4.3 %slice-start.2 = ((s8[14155776]{0:T(1024)(128)(4,1)}), s8[4194304]{0:T(1024)(128)(4,1)S(1)}, s32[]{:S(2)}) async-start(s8[14155776]{0:T(1024)(128)(4,1)} %bitcast.88), calls=%async_computation.7 | async-start | bytes 8388608
  116.5 1.1 copy-start.1
  116.5 1.1 copy-start.4
  116.6 1.6 slice-start.3
  130.4 40.4 %all-to-all-start.3 = ((bf16[8,32,3072]{2,1,0:T(8,128)(2,1)}), bf16[8,32,3072]{2,1,0:T(8,128)(2,1)}, u32[]{:S(2)}, u32[]{:S(2)}) async-start(bf16[8,32,3072]{2,1,0:T(8,128)(2,1)} %copy.58), calls=%async_computation.3 | async-start | bytes 3145728 | tf_op jit(solution)/shard_map/all_to_all | solution.py:103
  176.3 6.0 %copy-start.9 = (s32[8]{0:T(128)S(1)}, s32[8]{0:T(128)}, u32[]{:S(2)}) copy-start(s32[8]{0:T(128)} %param.13) | copy-start | bytes 100
  177.8 20.9 %copy-start.7 = (pred[8,32]{1,0:T(8,128)(4,1)S(1)}, pred[8,32]{1,0:T(8,128)(4,1)}, u32[]{:S(2)}) copy-start(pred[8,32]{1,0:T(8,128)(4,1)} %copy-done.6) | copy-start | bytes 772
  178.7 19.6 %all-to-all-start.4 = ((bf16[8,32,1152]{2,1,0:T(8,128)(2,1)}), bf16[8,32,1152]{2,1,0:T(8,128)(2,1)S(1)}, u32[]{:S(2)}, u32[]{:S(2)}) async-start(bf16[8,32,1152]{2,1,0:T(8,128)(2,1)} %copy.64), calls=%async_computation.4 | async-start | bytes 1179648 | tf_op jit(solution)/shard_map/all_to_all | solution.py:106
  198.7 6.8 %copy-start.5 = (f32[1152]{0:T(1024)S(1)}, f32[1152]{0:T(1024)}, u32[]{:S(2)}) copy-start(f32[1152]{0:T(1024)} %param.22) | copy-start | bytes 13828
  204.6 0.9 copy-start.3
where the time goes:
time: 356 us
  blocking collectives  222 us (62%)
  waiting for transfers between devices  68.2 us (19%)
  matrix products  29 us (8%)
  starting transfers between devices  19.7 us (6%)
  local copies, waits for them, and re-layouts  9.53 us (3%)
  other arithmetic  6.06 us (2%)
    all_to_all x1, blocking collectives, local(): lax.all_to_all(delta, 'ad', split_axis=0, concat_axis=0, tiled=True)  74.3 us
    all_gather x1, blocking collectives, local(): lax.all_gather(final, ('req', 'ad'), axis=0, tiled=True)  69.7 us
    psum x1, blocking collectives, local(): lax.psum(jnp.sum(jnp.exp(logits - highest[:, None]), axis=1), ('req', 'ad'))  41.3 us
    pmax x1, blocking collectives, local(): highest = lax.pmax(local_max, ('req', 'ad'))  36.9 us
    all_to_all x1, waiting for transfers between devices, local(): lax.all_to_all(place(hidden_kept), 'ad', split_axis=0, concat_axis=0, til...  35.1 us
    all_to_all x1, waiting for transfers between devices, local(): lax.all_to_all(delta, 'ad', split_axis=0, concat_axis=0, tiled=True)  16 us
    all_to_all x1, waiting for transfers between devices, local(): lax.all_to_all(place(kept), 'ad', split_axis=0, concat_axis=0, tiled=True)  15.5 us
    all_to_all x1, starting transfers between devices, local(): lax.all_to_all(slot_rows, 'ad', split_axis=0, concat_axis=0, tiled=True)  7.25 us
  transfers between devices with their start and end apart: 4, of which 4 were waited for; matrix products, arithmetic and copies ran while one was open for 2% of the time, Pallas kernels for 0%

commit v1 on v0

v1 whole, which is shorter than its diff:
```python
import functools

import jax
import jax.numpy as jnp
from jax import lax
from jax.experimental import pallas as pl
from jax.experimental.pallas import tpu as pltpu
from jax.sharding import PartitionSpec as P

epsilon = 1e-05
MESH = pl.DeviceIdType.MESH
VMEM_SPEC = pl.BlockSpec(memory_space=pltpu.VMEM)
SMEM_SPEC = pl.BlockSpec(memory_space=pltpu.SMEM)


def rms_scale(values, gain):
    mean_sq = jnp.mean(values * values, axis=-1, keepdims=True)
    return values * lax.rsqrt(mean_sq + epsilon) * gain


def dispatch_kernel(
    groups, per_dev, ids_ref, len_ref, x_ref, rows_ref, meta_ref,
    stage, mstage, local_sem, send_sem, recv_sem, msend_sem, mrecv_sem,
):
    q = lax.axis_index("req")
    me = lax.axis_index("ad")
    n_req = x_ref.shape[0]
    barrier = pltpu.get_barrier_semaphore()

    def greet(k, carry):
        pl.semaphore_signal(
            barrier, inc=1, device_id=(q, lax.rem(me + k, groups)), device_id_type=MESH
        )
        return carry

    lax.fori_loop(1, groups, greet, 0)
    lane = lax.broadcasted_iota(jnp.int32, (8, 128), 1)

    def fill(h, carry):
        pick = jnp.int32(-1)
        code = jnp.int32(0)
        size = jnp.int32(0)
        for r in range(n_req):
            a = ids_ref[r]
            hit = lax.div(a, per_dev) == h
            pick = jnp.where(hit, r, pick)
            code = jnp.where(hit, lax.rem(a, per_dev), code)
            size = jnp.where(hit, len_ref[r], size)
        stage[h] = x_ref[jnp.maximum(pick, 0)]
        mstage[h] = jnp.where(lane == 0, code, jnp.where(lane == 1, size, pick))
        return carry

    lax.fori_loop(0, groups, fill, 0)
    own = pltpu.make_async_copy(stage.at[me], rows_ref.at[me], local_sem.at[0])
    own_meta = pltpu.make_async_copy(mstage.at[me], meta_ref.at[me], local_sem.at[1])
    own.start()
    own_meta.start()
    pl.semaphore_wait(barrier, groups - 1)

    def pair(k):
        h = lax.rem(me + k, groups)
        rows = pltpu.make_async_remote_copy(
            src_ref=stage.at[h], dst_ref=rows_ref.at[me],
            send_sem=send_sem.at[k], recv_sem=recv_sem.at[k],
            device_id=(q, h), device_id_type=MESH,
        )
        meta = pltpu.make_async_remote_copy(
            src_ref=mstage.at[h], dst_ref=meta_ref.at[me],
            send_sem=msend_sem.at[k], recv_sem=mrecv_sem.at[k],
            device_id=(q, h), device_id_type=MESH,
        )
        return rows, meta

    def start(k, carry):
        rows, meta = pair(k)
        meta.start()
        rows.start()
        return carry

    def finish(k, carry):
        rows, meta = pair(k)
        meta.wait()
        rows.wait()
        return carry

    lax.fori_loop(1, groups, start, 0)
    lax.fori_loop(1, groups, finish, 0)
    own.wait()
    own_meta.wait()


def dispatch(residual, lengths, adapter_ids, groups, per_dev):
    n_req, seq, width = residual.shape
    dma = pltpu.SemaphoreType.DMA
    return pl.pallas_call(
        functools.partial(dispatch_kernel, groups, per_dev),
        out_shape=(
            jax.ShapeDtypeStruct((groups, seq, width), residual.dtype),
            jax.ShapeDtypeStruct((groups, 8, 128), jnp.int32),
        ),
        in_specs=[SMEM_SPEC, SMEM_SPEC, VMEM_SPEC],
        out_specs=(VMEM_SPEC, VMEM_SPEC),
        scratch_shapes=[
            pltpu.VMEM((groups, seq, width), residual.dtype),
            pltpu.VMEM((groups, 8, 128), jnp.int32),
            dma((2,)), dma((groups,)), dma((groups,)), dma((groups,)), dma((groups,)),
        ],
        compiler_params=pltpu.CompilerParams(
            collective_id=0, has_side_effects=True, vmem_limit_bytes=16 << 20
        ),
    )(adapter_ids, lengths, residual)


def head_kernel(
    n_req_axis, groups, per_dev, ids_ref, fin_ref, y_ref, w_ref, out_ref, lp_ref,
    gathered, wide, back, stats, own_stats, local_sem,
    fsend, frecv, ysend, yrecv, ssend, srecv,
):
    q = lax.axis_index("req")
    a = lax.axis_index("ad")
    n = n_req_axis * groups
    me = q * groups + a
    n_req = out_ref.shape[0]
    width = out_ref.shape[2]
    total_req = lp_ref.shape[0]
    slots = n * groups
    barrier = pltpu.get_barrier_semaphore()

    def target(k):
        t = lax.rem(me + k, n)
        return (lax.div(t, groups), lax.rem(t, groups))

    def greet(k, carry):
        pl.semaphore_signal(barrier, inc=1, device_id=target(k), device_id_type=MESH)
        return carry

    lax.fori_loop(1, n, greet, 0)
    gathered[me] = fin_ref[...]
    own = pltpu.make_async_copy(y_ref.at[a], back.at[a], local_sem)
    own.start()
    pl.semaphore_wait(barrier, n - 1)

    def fin_copy(k):
        return pltpu.make_async_remote_copy(
            src_ref=fin_ref, dst_ref=gathered.at[me],
            send_sem=fsend.at[k], recv_sem=frecv.at[k],
            device_id=target(k), device_id_type=MESH,
        )

    def row_copy(k):
        h = lax.rem(a + k, groups)
        return pltpu.make_async_remote_copy(
            src_ref=y_ref.at[h], dst_ref=back.at[a],
            send_sem=ysend.at[k], recv_sem=yrecv.at[k],
            device_id=(q, h), device_id_type=MESH,
        )

    def stat_copy(k):
        return pltpu.make_async_remote_copy(
            src_ref=own_stats, dst_ref=stats.at[me],
            send_sem=ssend.at[k], recv_sem=srecv.at[k],
            device_id=target(k), device_id_type=MESH,
        )

    def start_all(copy, count):
        def body(k, carry):
            copy(k).start()
            return carry
        lax.fori_loop(1, count, body, 0)

    def wait_all(copy, count):
        def body(k, carry):
            copy(k).wait()
            return carry
        lax.fori_loop(1, count, body, 0)

    start_all(fin_copy, n)
    start_all(row_copy, groups)
    wait_all(fin_copy, n)

    def widen(d, carry):
        at = pl.multiple_of(d * groups, 8)
        wide[pl.ds(at, groups), :] = gathered[d].astype(jnp.float32)
        return carry

    lax.fori_loop(0, n, widen, 0)
    picked = jnp.transpose(wide[:, width:])[0:1, :].astype(jnp.int32)
    slot = lax.broadcasted_iota(jnp.int32, (1, slots), 1)
    req_of = lax.div(slot, groups * groups)
    source = lax.rem(slot, groups)
    row_id = (req_of * groups + source) * n_req + picked
    row_id = jnp.where(picked >= 0, row_id, -1)
    want = lax.broadcasted_iota(jnp.int32, (total_req, slots), 0)
    place = jnp.where(want == row_id, 1.0, 0.0).astype(jnp.bfloat16)
    ordered = jnp.dot(
        place, wide[:, :width].astype(jnp.bfloat16), preferred_element_type=jnp.float32
    ).astype(jnp.bfloat16)
    logits = jnp.dot(ordered, w_ref[...], preferred_element_type=jnp.float32)
    lp_ref[...] = logits
    top = jnp.max(logits, axis=1, keepdims=True)
    part = jnp.sum(jnp.exp(logits - top), axis=1, keepdims=True)
    own_stats[0:1, :] = jnp.transpose(jnp.broadcast_to(top, (total_req, 128)))[0:1, :]
    own_stats[1:2, :] = jnp.transpose(jnp.broadcast_to(part, (total_req, 128)))[0:1, :]
    start_all(stat_copy, n)
    stats[me] = own_stats[...]

    wait_all(row_copy, groups)
    own.wait()
    for r in range(n_req):
        out_ref[r] = back[lax.div(ids_ref[r], per_dev)]

    wait_all(stat_copy, n)
    tops = stats[:, 0, :]
    best = jnp.max(tops, axis=0, keepdims=True)
    total = jnp.sum(stats[:, 1, :] * jnp.exp(tops - best), axis=0, keepdims=True)
    best_col = jnp.transpose(jnp.broadcast_to(best, (128, total_req)))[:, 0:1]
    log_col = jnp.transpose(jnp.broadcast_to(jnp.log(total), (128, total_req)))[:, 0:1]
    lp_ref[...] = lp_ref[...] - best_col - log_col


def head(adapter_ids, final, y, head_weight, n_req, total_req, n_req_axis, groups, per_dev):
    n = n_req_axis * groups
    seq, width = y.shape[1:]
    dma = pltpu.SemaphoreType.DMA
    return pl.pallas_call(
        functools.partial(head_kernel, n_req_axis, groups, per_dev),
        out_shape=(
            jax.ShapeDtypeStruct((n_req, seq, width), y.dtype),
            jax.ShapeDtypeStruct((total_req, head_weight.shape[1]), jnp.float32),
        ),
        in_specs=[SMEM_SPEC, VMEM_SPEC, VMEM_SPEC, VMEM_SPEC],
        out_specs=(VMEM_SPEC, VMEM_SPEC),
        scratch_shapes=[
            pltpu.VMEM((n, groups, width + 128), jnp.bfloat16),
            pltpu.VMEM((n * groups, width + 128), jnp.float32),
            pltpu.VMEM((groups, seq, width), y.dtype),
            pltpu.VMEM((n, 2, total_req), jnp.float32),
            pltpu.VMEM((2, total_req), jnp.float32),
            dma(()), dma((n,)), dma((n,)), dma((groups,)), dma((groups,)), dma((n,)), dma((n,)),
        ],
        compiler_params=pltpu.CompilerParams(
            collective_id=1, has_side_effects=True, vmem_limit_bytes=56 << 20
        ),
    )(adapter_ids, final, y, head_weight)


def local(
    residual,
    lengths,
    adapter_ids,
    ffn_gain,
    w_gate_up,
    w_down,
    adapter_input_first,
    ad_out_b,
    ad_down_a,
    adapter_down_second,
    final_gain,
    head_weight,
):
    n_req, seq, width = residual.shape
    groups = lax.axis_size("ad")
    n_req_axis = lax.axis_size("req")
    per_dev = adapter_input_first.shape[0]
    rank = ad_down_a.shape[1]
    units = w_down.shape[0]
    f32 = jnp.float32
    rows, meta = dispatch(residual, lengths, adapter_ids, groups, per_dev)
    slot_id = meta[:, 0, 0]
    slot_len = meta[:, 0, 1]
    slot_req = meta[:, 0, 2]
    positions = jnp.arange(seq, dtype=jnp.int32)
    flat = rows.reshape(groups * seq, width)
    row_id = jnp.repeat(slot_id, seq)[:, None]
    valid = (positions[None, :] < slot_len[:, None]).reshape(groups * seq, 1)
    stream = flat.astype(f32)
    normed = rms_scale(stream, ffn_gain).astype(jnp.bfloat16)
    in_a = adapter_input_first.reshape(per_dev * 2 * rank, width)
    low = lax.dot_general(normed, in_a, (((1,), (1,)), ((), ())), preferred_element_type=f32)
    lane = jnp.arange(per_dev * 2 * rank, dtype=jnp.int32)[None, :]
    mine = lane // (2 * rank) == row_id
    half = lane % (2 * rank) < rank
    low_gate = jnp.where(mine & half, low, 0.0).astype(jnp.bfloat16)
    low_up = jnp.where(mine & ~half, low, 0.0).astype(jnp.bfloat16)
    out_b = ad_out_b.reshape(per_dev * 2 * rank, units)

    def widened(base, lowered):
        return jnp.dot(normed, base, preferred_element_type=f32) + jnp.dot(
            lowered, out_b, preferred_element_type=f32
        )

    gate = widened(w_gate_up[0], low_gate)
    up_part = widened(w_gate_up[1], low_up)
    hidden = (jax.nn.silu(gate) * up_part).astype(jnp.bfloat16)
    down_a = ad_down_a.reshape(per_dev * rank, units)
    low_d = lax.dot_general(hidden, down_a, (((1,), (1,)), ((), ())), preferred_element_type=f32)
    lane_d = jnp.arange(per_dev * rank, dtype=jnp.int32)[None, :]
    low_d = jnp.where(lane_d // rank == row_id, low_d, 0.0).astype(jnp.bfloat16)
    mixed = (
        stream
        + jnp.dot(hidden, w_down, preferred_element_type=f32)
        + jnp.dot(low_d, adapter_down_second.reshape(per_dev * rank, width), preferred_element_type=f32)
    )
    y = jnp.where(valid, mixed, 0.0).astype(jnp.bfloat16).reshape(groups, seq, width)
    is_last = (positions[None, :] == slot_len[:, None] - 1)[..., None]
    last = jnp.sum(jnp.where(is_last, y.astype(f32), 0.0), axis=1)
    final = rms_scale(last, final_gain).astype(jnp.bfloat16)
    tag = jnp.broadcast_to(slot_req[:, None], (groups, 128)).astype(jnp.bfloat16)
    final = jnp.concatenate([final, tag], axis=1)
    return head(
        adapter_ids, final, y, head_weight, n_req, n_req * n_req_axis * groups,
        n_req_axis, groups, per_dev,
    )


def solution(mesh):
    in_specs = (
        P(("req", "ad"), None, None),
        P(("req", "ad")),
        P(("req", "ad")),
        P(),
        P(),
        P(),
        P("ad", None, None),
        P("ad", None, None, None),
        P("ad", None, None),
        P("ad", None, None),
        P(),
        P(None, ("req", "ad")),
    )
    out_specs = (P(("req", "ad"), None, None), P(None, ("req", "ad")))
    return jax.shard_map(local, mesh=mesh, in_specs=in_specs, out_specs=out_specs, check_vma=False)
```

time: 356 us -> 97.7 us (0.27)
  blocking collectives: 222 us -> 0 us
  waiting for transfers between devices: 68.2 us -> 0 us
  Pallas kernels: 0 us -> 59.8 us
  starting transfers between devices: 19.7 us -> 0 us
  matrix products: 29 us -> 24.2 us
  other arithmetic: 6.06 us -> 2.45 us
    all_to_all x1 -> x0, blocking collectives: 74.3 us -> none  [local(): lax.all_to_all(delta, 'ad', split_axis=0, concat_axis=0, tiled=True)]
    all_gather x1 -> x0, blocking collectives: 69.7 us -> none  [local(): lax.all_gather(final, ('req', 'ad'), axis=0, tiled=True)]
    all_to_all x4 -> x0, waiting for transfers between devices: 68.2 us -> none  [the longest x1 35.1 us: local(): lax.all_to_all(place(hidden_kept), 'ad', split_axis=0, concat_axis=0, til...]
    pallas_call x0 -> x2, Pallas kernels: none -> 59.8 us  [the longest x1 42.9 us: head(): pl.pallas_call(functools.partial(head_kernel, n_req_axis, groups, per_dev...]
    psum x1 -> x0, blocking collectives: 41.3 us -> none  [local(): lax.psum(jnp.sum(jnp.exp(logits - highest[:, None]), axis=1), ('req', 'ad'))]
    pmax x1 -> x0, blocking collectives: 36.9 us -> none  [local(): highest = lax.pmax(local_max, ('req', 'ad'))]
    all_to_all x4 -> x0, starting transfers between devices: 19.7 us -> none  [the longest x1 7.25 us: local(): lax.all_to_all(slot_rows, 'ad', split_axis=0, concat_axis=0, tiled=True)]
    unnamed x30 -> x26, local copies, waits for them, and re-layouts: 1 us -> 6.92 us
  transfers between devices with their start and end apart: 4 -> 0, of which waited for: 4 -> 0; matrix products, arithmetic and copies ran while one was open for 2% -> 0% of each run, Pallas kernels for 0% -> 0%
where the time goes in v1:
time: 97.7 us; the launch traced here: 97.4 us
  Pallas kernels  59.8 us (61%)
  matrix products  24.2 us (25%)
  local copies, waits for them, and re-layouts  10.1 us (10%)
  other arithmetic  2.45 us (3%)
    pallas_call x1, Pallas kernels, head(): pl.pallas_call(functools.partial(head_kernel, n_req_axis, groups, per_dev...  42.9 us
    pallas_call x1, Pallas kernels, dispatch(): pl.pallas_call(functools.partial(dispatch_kernel, groups, per_dev), out_s...  16.8 us
    dot_general x2, matrix products, widened(): jnp.dot(normed, base, preferred_element_type=f32)  11 us
    unnamed x26, local copies, waits for them, and re-layouts  6.92 us
    dot_general x2, matrix products, widened(): jnp.dot(lowered, out_b, preferred_element_type=f32)  5.84 us
    dot_general x1, matrix products, local(): jnp.dot(low_d, adapter_down_second.reshape(per_dev * rank, width), prefer...  3.83 us
    dot_general x1, matrix products, local(): jnp.dot(hidden, w_down, preferred_element_type=f32)  3.24 us
    pallas_call x1, local copies, waits for them, and re-layouts, head(): pl.pallas_call(functools.partial(head_kernel, n_req_axis, groups, per_dev...  2.51 us

profile of v1, /device:TPU:0, one launch (start us, length us, event | category | flops | bytes accessed | tf_op | source)
XLA Modules:
  0.0 97.4 jit_solution(1180329290349651040)
XLA Ops:
  0.7 1.1 %copy-done.1 = bf16[8,32,1152]{2,1,0:T(8,128)(2,1)S(1)} copy-done((bf16[8,32,1152]{2,1,0:T(8,128)(2,1)S(1)}, bf16[8,32,1152]{2,1,0:T(8,128)(2,1)}, u32[]{:S(2)}) %copy-start.1) | copy-done | bytes 589848
  1.8 0.7 copy-done.2
  2.4 0.7 copy-done.3
  3.1 16.8 %shard_map.131 = (bf16[8,32,1152]{2,1,0:T(8,128)(2,1)S(1)}, s32[8,8,128]{2,1,0:T(8,128)S(1)}) custom-call(s32[8]{0:T(128)S(1)} %copy-done.2, s32[8]{0:T(128)S(1)} %copy-done.3, bf16[8,32,1152]{2,1,0:T(8,128)(2,1)S(1)} %copy-done.1), custom_call_target="tpu_custom_call" | custom-call | tf_op jit(solution)/shard_map/pallas_call | solution.py:95
  20.0 0.2 fusion.23
  20.2 0.4 slice_reduce_fusion
  20.7 0.2 multiply_reduce_fusion
  20.9 1.0 %multiply_convert_fusion = bf16[8,32,1152]{2,1,0:T(8,128)(2,1)S(1)} fusion(bf16[8,32,1152]{2,1,0:T(8,128)(2,1)S(1)} %get-tuple-element.5, f32[1152]{0:T(1024)} %param.15, f32[8,32]{1,0:T(8,128)S(1)} %add_rsqrt_fusion), kind=kLoop, calls=%fused_computation.15 | loop fusion | flops 1179648 | bytes 1185280 | tf_op jit(solution)/shard_map/convert_element_type | solution.py:277
  22.0 7.1 %fusion = f32[256,3072]{1,0:T(8,128)} fusion(bf16[256,1152]{1,0:T(8,128)(2,1)S(1)} %bitcast.30, bf16[2,1152,3072]{2,1,0:T(8,128)(2,1)} %param.16), kind=kOutput, calls=%fused_computation | convolution fusion | flops 1811939328 | bytes 10813440 | tf_op jit(solution)/shard_map/dot_general | solution.py:288
  29.1 3.9 %fusion.2 = f32[256,3072]{1,0:T(8,128)} fusion(bf16[256,1152]{1,0:T(8,128)(2,1)S(1)} %bitcast.31, bf16[2,1152,3072]{2,1,0:T(8,128)(2,1)S(1)} %copy-done.9), kind=kOutput, calls=%fused_computation.2 | convolution fusion | flops 1811939328 | bytes 10813440 | tf_op jit(solution)/shard_map/dot_general | solution.py:288
  33.0 0.3 fusion.29
  33.4 0.1 eq.54
  33.5 2.7 %convolution_add_fusion.1 = f32[256,3072]{1,0:T(8,128)S(1)} fusion(f32[256,3072]{1,0:T(8,128)} %fusion.2, bf16[128,3072]{1,0:T(8,128)(2,1)S(1)} %bitcast.26, bf16[256,128]{1,0:T(8,128)(2,1)S(1)} %fusion.29, s32[128]{0:T(128)S(1)} %and_select_fusion.2, s32[256]{0:T(256)S(1)} %eq.54, pred[128]{0:T(512)(128)(4,1)S(1)} %fusion.24), kind=kOutput, calls=%fused_computation.8 | convolution fusion | flops 202211328 | bytes 7145088 | tf_op jit(solution)/shard_map/dot_general | solution.py:288
  36.2 3.2 %fusion.7 = bf16[256,3072]{1,0:T(8,128)(2,1)S(1)} fusion(f32[256,3072]{1,0:T(8,128)} %fusion, bf16[128,3072]{1,0:T(8,128)(2,1)S(1)} %bitcast.27, f32[256,3072]{1,0:T(8,128)S(1)} %convolution_add_fusion.1, bf16[256,128]{1,0:T(8,128)(2,1)S(1)} %fusion.29, s32[128]{0:T(128)S(1)} %and_select_fusion.2, s32[256]{0:T(256)S(1)} %eq.54, pred[128]{0:T(512)(128)(4,1)S(1)} %fusion.25), kind=kOutput, calls=%fused_computation.9 | convolution fusion | flops 206929920 | bytes 8717952 | tf_op jit(solution)/shard_map/dot_general | solution.py:288
  39.4 3.2 %convolution_add_fusion.3 = f32[256,1152]{1,0:T(8,128)} fusion(bf16[256,3072]{1,0:T(8,128)(2,1)S(1)} %fusion.7, bf16[3072,1152]{1,0:T(8,128)(2,1)S(1)} %bitcast.37, bf16[256,1152]{1,0:T(8,128)(2,1)S(1)} %bitcast.28), kind=kOutput, calls=%fused_computation.12 | convolution fusion | flops 1812529152 | bytes 10420224 | tf_op jit(solution)/shard_map/dot_general | solution.py:301
  42.7 0.1 lt.44
  42.8 3.8 %select_reduce_fusion = (f32[8,1152]{1,0:T(8,128)S(1)}, bf16[256,1152]{1,0:T(8,128)(2,1)}) fusion(pred[8,32]{1,0:T(8,128)(4,1)S(1)} %iota_compare_fusion.1, f32[256,1152]{1,0:T(8,128)} %convolution_add_fusion.3, bf16[64,1152]{1,0:T(8,128)(2,1)} %bitcast.35, bf16[256,3072]{1,0:T(8,128)(2,1)} %copy-done.5, bf16[64,3072]{1,0:T(8,128)(2,1)S(1)} %bitcast.33, ...), kind=kOutput, calls=%fused_computation.14 | convolution fusion | flops 140221440 | bytes 3921664 | tf_op jit(solution)/shard_map/dot_general | solution.py:302
  46.7 0.1 multiply_reduce_fusion.1
  46.8 0.1 multiply_convert_fusion.1
  46.9 0.6 pad_maximum_fusion.fin_ref
  47.5 2.5 %copy.16.w_ref = bf16[1152,1000]{1,0:T(8,128)(2,1)} copy(bf16[1152,1000]{0,1:T(8,128)(2,1)S(1)} %copy-done.4) | data formatting | bytes 4608000 | tf_op args[11]
  50.0 42.9 %shard_map.132 = (bf16[8,32,1152]{2,1,0:T(8,128)(2,1)}, f32[256,1000]{1,0:T(8,128)}) custom-call(s32[8]{0:T(128)} %ids_ref.3, bf16[8,1280]{1,0:T(8,128)(2,1)} %pad_maximum_fusion.fin_ref, bf16[8,32,1152]{2,1,0:T(8,128)(2,1)} %bitcast.29, bf16[1152,1000]{1,0:T(8,128)(2,1)} %copy.16.w_ref), custom_call_target="tpu_custom_call" | custom-call | tf_op jit(solution)/shard_map/pallas_call | solution.py:225
  92.9 2.5 %copy.17 = f32[256,1000]{0,1:T(8,128)} copy(f32[256,1000]{1,0:T(8,128)} %get-tuple-element.9) | data formatting | bytes 2048000 | tf_op jit(solution)/shard_map/pallas_call | solution.py:225
  95.4 1.9 %copy.19 = bf16[8,32,1152]{2,1,0:T(8,128)(2,1)} copy(bf16[8,32,1152]{2,1,0:T(8,128)(2,1)} %get-tuple-element.16) | data formatting | bytes 1179648
  (33 shorter events, 0.4 us)
Async XLA Ops:
  0.6 28.5 %copy-start = (bf16[4,2,16,3072]{3,2,1,0:T(8,128)(2,1)S(1)}, bf16[4,2,16,3072]{3,2,1,0:T(8,128)(2,1)}, u32[]{:S(2)}) copy-start(bf16[4,2,16,3072]{3,2,1,0:T(8,128)(2,1)} %param.19) | copy-start | bytes 2359300
  0.6 1.1 %copy-start.1 = (bf16[8,32,1152]{2,1,0:T(8,128)(2,1)S(1)}, bf16[8,32,1152]{2,1,0:T(8,128)(2,1)}, u32[]{:S(2)}) copy-start(bf16[8,32,1152]{2,1,0:T(8,128)(2,1)} %x_ref.1) | copy-start | bytes 1769476
  1.8 0.7 copy-start.2
  2.4 0.7 copy-start.3
  20.9 8.2 %copy-start.9 = (bf16[2,1152,3072]{2,1,0:T(8,128)(2,1)S(1)}, bf16[2,1152,3072]{2,1,0:T(8,128)(2,1)}, u32[]{:S(2)}) copy-start(bf16[2,1152,3072]{2,1,0:T(8,128)(2,1)} %param.16) | copy-start | bytes 42467332
  29.1 3.9 %copy-start.7 = (bf16[4,32,1152]{2,1,0:T(8,128)(2,1)S(1)}, bf16[4,32,1152]{2,1,0:T(8,128)(2,1)}, u32[]{:S(2)}) copy-start(bf16[4,32,1152]{2,1,0:T(8,128)(2,1)} %param.18) | copy-start | bytes 884740
  33.5 5.9 %slice-start = ((s8[7077888]{0:T(1024)(128)(4,1)}), s8[4194304]{0:T(1024)(128)(4,1)S(1)}, s32[]{:S(2)}) async-start(s8[7077888]{0:T(1024)(128)(4,1)} %bitcast.36), calls=%async_computation | async-start | bytes 8388608
  36.2 3.2 %slice-start.1 = ((s8[7077888]{0:T(1024)(128)(4,1)}), s8[2883584]{0:T(1024)(128)(4,1)S(1)}, s32[]{:S(2)}) async-start(s8[7077888]{0:T(1024)(128)(4,1)} %bitcast.36), calls=%async_computation.1 | async-start | bytes 5767168
  39.4 3.3 %copy-start.5 = (bf16[256,3072]{1,0:T(8,128)(2,1)}, bf16[256,3072]{1,0:T(8,128)(2,1)S(1)}, u32[]{:S(2)}) copy-start(bf16[256,3072]{1,0:T(8,128)(2,1)S(1)} %fusion.7) | copy-start | bytes 4718596
  39.4 3.4 %copy-start.6 = (bf16[4,16,3072]{2,1,0:T(8,128)(2,1)S(1)}, bf16[4,16,3072]{2,1,0:T(8,128)(2,1)}, u32[]{:S(2)}) copy-start(bf16[4,16,3072]{2,1,0:T(8,128)(2,1)} %param.20) | copy-start | bytes 1179652
  42.7 4.1 %copy-start.8 = (f32[1152]{0:T(1024)S(1)}, f32[1152]{0:T(1024)}, u32[]{:S(2)}) copy-start(f32[1152]{0:T(1024)} %param.22) | copy-start | bytes 13828
  42.7 4.8 %copy-start.4 = (bf16[1152,1000]{0,1:T(8,128)(2,1)S(1)}, bf16[1152,1000]{0,1:T(8,128)(2,1)}, u32[]{:S(2)}) copy-start(bf16[1152,1000]{0,1:T(8,128)(2,1)} %param.23) | copy-start | bytes 6912004

commit v2 on v0

v2 whole, which is shorter than its diff:
```python
import functools

import jax
import jax.numpy as jnp
from jax import lax
from jax.experimental import pallas as pl
from jax.experimental.pallas import tpu as pltpu
from jax.sharding import PartitionSpec as P

epsilon = 1e-05
CHUNKS = 1
MESH = pl.DeviceIdType.MESH
VMEM_SPEC = pl.BlockSpec(memory_space=pltpu.VMEM)
ANY_SPEC = pl.BlockSpec(memory_space=pl.ANY)
NT = (((1,), (1,)), ((), ()))


def layer_kernel(
    n_q, groups, per_dev, n_req,
    ids_hbm, len_hbm, x_hbm, gain_ref, fgain_ref, wgu_hbm, wd_hbm, ina_hbm, outb_hbm,
    downa_hbm, downb_hbm, wh_hbm,
    back, lt_ref, lse_ref,
    ids, lens, xs, stage, mstage, recv, mrecv, normed, low_g, low_u, hidden, mixed, y, last,
    wgu, wd, ina, outb, downa, downb, wh,
    fin, gathered, wide, stats, own_stats,
    isem, wsem, lsem, rsend, rrecv, msend, mrec, ysend, yrecv,
    fsend, frecv, gsend, grecv, ssend, srecv,
):
    f32 = jnp.float32
    bf16 = jnp.bfloat16
    q = lax.axis_index("req")
    a = lax.axis_index("ad")
    n = n_q * groups
    me = q * groups + a
    seq, width = xs.shape[1:]
    rank = downa.shape[0] // per_dev
    units = wd.shape[0]
    slots = n * groups
    total_req = n * n_req
    barrier = pltpu.get_barrier_semaphore()

    def target(k):
        t = lax.rem(me + k, n)
        return (lax.div(t, groups), lax.rem(t, groups))

    firsts = [
        pltpu.make_async_copy(ids_hbm, ids, isem.at[0]),
        pltpu.make_async_copy(len_hbm, lens, isem.at[1]),
        pltpu.make_async_copy(x_hbm, xs, isem.at[2]),
    ]
    for copy in firsts:
        copy.start()

    def greet(k, carry):
        pl.semaphore_signal(barrier, inc=1, device_id=target(k), device_id_type=MESH)
        return carry

    lax.fori_loop(1, n, greet, 0)
    part = width // 4
    loads = [pltpu.make_async_copy(ina_hbm, ina, wsem.at[0])]
    for j in range(2):
        for c in range(4):
            rows = pl.ds(c * part, part)
            loads.append(
                pltpu.make_async_copy(
                    wgu_hbm.at[j, rows], wgu.at[j, rows], wsem.at[1 + 4 * j + c]
                )
            )
    loads.append(pltpu.make_async_copy(outb_hbm, outb, wsem.at[9]))
    early = len(loads)
    loads.append(pltpu.make_async_copy(downa_hbm, downa, wsem.at[10]))
    loads.append(pltpu.make_async_copy(downb_hbm, downb, wsem.at[11]))
    for c in range(2):
        rows = pl.ds(c * (units // 2), units // 2)
        loads.append(pltpu.make_async_copy(wd_hbm.at[rows], wd.at[rows], wsem.at[12 + c]))
    later = len(loads)
    loads.append(pltpu.make_async_copy(wh_hbm, wh, wsem.at[14]))
    for copy in firsts:
        copy.wait()
    for copy in loads:
        copy.start()

    line = lax.broadcasted_iota(jnp.int32, (8, 128), 0)

    def fill(k, carry):
        h = lax.rem(a + k, groups)
        pick = jnp.int32(-1)
        code = jnp.int32(0)
        size = jnp.int32(0)
        for r in range(n_req):
            i = ids[r]
            hit = lax.div(i, per_dev) == h
            pick = jnp.where(hit, r, pick)
            code = jnp.where(hit, lax.rem(i, per_dev), code)
            size = jnp.where(hit, lens[r], size)
        stage[k] = xs[jnp.maximum(pick, 0)]
        mstage[k] = jnp.where(line == 0, code, jnp.where(line == 1, size, pick))
        return carry

    lax.fori_loop(0, groups, fill, 0)
    pl.semaphore_wait(barrier, n - 1)

    def row_copy(k):
        return pltpu.make_async_remote_copy(
            src_ref=stage.at[k], dst_ref=recv.at[k],
            send_sem=rsend.at[k], recv_sem=rrecv.at[k],
            device_id=(q, lax.rem(a + k, groups)), device_id_type=MESH,
        )

    def meta_copy(k):
        return pltpu.make_async_remote_copy(
            src_ref=mstage.at[k], dst_ref=mrecv.at[k],
            send_sem=msend.at[k], recv_sem=mrec.at[k],
            device_id=(q, lax.rem(a + k, groups)), device_id_type=MESH,
        )

    def back_copy(k):
        return pltpu.make_async_remote_copy(
            src_ref=y.at[k], dst_ref=back.at[a],
            send_sem=ysend.at[k], recv_sem=yrecv.at[k],
            device_id=(q, lax.rem(a + groups - k, groups)), device_id_type=MESH,
        )

    def start_rows(k, carry):
        meta_copy(k).start()
        row_copy(k).start()
        return carry

    lax.fori_loop(1, groups, start_rows, 0)
    recv[0] = stage[0]
    mrecv[0] = mstage[0]
    gain = gain_ref[...].reshape(1, width)
    lane = lax.broadcasted_iota(jnp.int32, (seq, per_dev * 2 * rank), 1)
    lane_d = lax.broadcasted_iota(jnp.int32, (seq, per_dev * rank), 1)
    group_of = lax.div(lane, 2 * rank)
    is_gate = lax.rem(lane, 2 * rank) < rank
    row_at = lax.broadcasted_iota(jnp.int32, (seq, width), 0)
    per = groups // CHUNKS
    size = per * seq
    tile_f = 512
    tile_d = width // 3
    own_back = pltpu.make_async_copy(y.at[0], back.at[a], lsem)

    for chunk in range(CHUNKS):
        mine = range(chunk * per, (chunk + 1) * per)
        for s in mine:
            if s > 0:
                meta_copy(s).wait_recv()
                row_copy(s).wait_recv()
            v = recv[s].astype(f32)
            mean_sq = jnp.mean(v * v, axis=-1, keepdims=True)
            at = (s - chunk * per) * seq
            normed[at : at + seq, :] = (v * lax.rsqrt(mean_sq + epsilon) * gain).astype(bf16)
        if chunk == 0:
            for copy in loads[:early]:
                copy.wait()
        low = lax.dot_general(normed[...], ina[...], NT, preferred_element_type=f32)
        for s in mine:
            at = (s - chunk * per) * seq
            here = group_of == mrecv[s, 0:1, : lane.shape[1]]
            piece = low[at : at + seq]
            low_g[at : at + seq, :] = jnp.where(here & is_gate, piece, 0.0).astype(bf16)
            low_u[at : at + seq, :] = jnp.where(
                here & jnp.logical_not(is_gate), piece, 0.0
            ).astype(bf16)

        def units_step(j, carry):
            cols = pl.ds(pl.multiple_of(j * tile_f, tile_f), tile_f)
            gate = jnp.dot(normed[...], wgu[0, :, cols], preferred_element_type=f32)
            gate = gate + jnp.dot(low_g[...], outb[:, cols], preferred_element_type=f32)
            up = jnp.dot(normed[...], wgu[1, :, cols], preferred_element_type=f32)
            up = up + jnp.dot(low_u[...], outb[:, cols], preferred_element_type=f32)
            hidden[:, cols] = (gate / (1.0 + jnp.exp(-gate)) * up).astype(bf16)
            return carry

        lax.fori_loop(0, units // tile_f, units_step, 0)
        if chunk == 0:
            for copy in loads[early:later]:
                copy.wait()
        low_d = lax.dot_general(hidden[...], downa[...], NT, preferred_element_type=f32)
        pieces = []
        for s in mine:
            at = (s - chunk * per) * seq
            here = lax.div(lane_d, rank) == mrecv[s, 0:1, : lane_d.shape[1]]
            pieces.append(jnp.where(here, low_d[at : at + seq], 0.0))
        low_d = jnp.concatenate(pieces, axis=0).astype(bf16)
        low_g[:, : lane_d.shape[1]] = low_d

        def width_step(j, carry):
            cols = pl.ds(pl.multiple_of(j * tile_d, tile_d), tile_d)
            mixed[:, cols] = jnp.dot(
                hidden[...], wd[:, cols], preferred_element_type=f32
            ) + jnp.dot(
                low_g[:, : lane_d.shape[1]], downb[:, cols], preferred_element_type=f32
            )
            return carry

        lax.fori_loop(0, width // tile_d, width_step, 0)
        for s in mine:
            at = (s - chunk * per) * seq
            length = mrecv[s, 1:2, 0:1]
            total = recv[s].astype(f32) + mixed[at : at + seq, :]
            out = jnp.where(row_at < length, total, 0.0).astype(bf16)
            y[s] = out
            last[s : s + 1, :width] = jnp.sum(
                jnp.where(row_at == length - 1, out.astype(f32), 0.0), axis=0, keepdims=True
            )
            last[s : s + 1, width:] = mrecv[s, 2:3, :].astype(f32)
        if chunk < CHUNKS - 1:
            for s in mine:
                if s > 0:
                    back_copy(s).start()
                else:
                    own_back.start()

    rows = last[:, :width]
    mean_sq = jnp.mean(rows * rows, axis=-1, keepdims=True)
    fin[:, :width] = (rows * lax.rsqrt(mean_sq + epsilon) * fgain_ref[...].reshape(1, width)).astype(bf16)
    fin[:, width:] = last[:, width:].astype(bf16)
    gathered[me] = fin[...]

    half = n // 2
    pairs = n_q // 2
    core = lax.rem(q, 2)
    sibling = (q + 1 - 2 * core, a)
    place_me = lax.div(q, 2) * groups + a

    def far(k):
        t = lax.rem(place_me + k, half)
        return (2 * lax.div(t, groups) + core, lax.rem(t, groups))

    def fin_copy(k):
        return pltpu.make_async_remote_copy(
            src_ref=fin, dst_ref=gathered.at[me],
            send_sem=fsend.at[k], recv_sem=frecv.at[k],
            device_id=far(k), device_id_type=MESH,
        )

    def pass_on(k):
        t = lax.rem(place_me + half - k, half)
        origin = (2 * lax.div(t, groups) + core) * groups + lax.rem(t, groups)
        return pltpu.make_async_remote_copy(
            src_ref=gathered.at[origin], dst_ref=gathered.at[origin],
            send_sem=gsend.at[k], recv_sem=grecv.at[k],
            device_id=sibling, device_id_type=MESH,
        )

    def stat_copy(k):
        return pltpu.make_async_remote_copy(
            src_ref=own_stats, dst_ref=stats.at[me],
            send_sem=ssend.at[k], recv_sem=srecv.at[k],
            device_id=target(k), device_id_type=MESH,
        )

    def each(low_k, high_k, action):
        def body(k, carry):
            action(k)
            return carry
        lax.fori_loop(low_k, high_k, body, 0)

    each(1, half, lambda k: fin_copy(k).start())
    pass_on(0).start()
    for s in range((CHUNKS - 1) * per, groups):
        if s > 0:
            back_copy(s).start()
        else:
            own_back.start()

    def relay(k):
        fin_copy(k).wait_recv()
        pass_on(k).start()

    each(1, half, relay)
    each(0, half, lambda k: pass_on(k).wait_recv())

    def widen(d):
        at = pl.multiple_of(d * groups, 8)
        wide[pl.ds(at, groups), :] = gathered[d].astype(f32)

    each(0, n, widen)
    picked = jnp.transpose(wide[:, width:])[0:1, :].astype(jnp.int32)
    slot = lax.broadcasted_iota(jnp.int32, (1, slots), 1)
    device = lax.div(slot, groups)
    holder = lax.rem(device, groups)
    source = lax.rem(holder + groups - lax.rem(slot, groups), groups)
    row_id = (lax.div(device, groups) * groups + source) * n_req + picked
    row_id = jnp.where(picked >= 0, row_id, -1)
    want = lax.broadcasted_iota(jnp.int32, (total_req, slots), 0)
    place = jnp.where(want == row_id, 1.0, 0.0).astype(bf16)
    ordered = jnp.dot(
        place, wide[:, :width].astype(bf16), preferred_element_type=f32
    ).astype(bf16)
    loads[later].wait()
    logits = lax.dot_general(wh[...], ordered, NT, preferred_element_type=f32)
    lt_ref[...] = logits
    top = jnp.max(logits, axis=0, keepdims=True)
    own_stats[0:1, :] = top
    own_stats[1:2, :] = jnp.sum(jnp.exp(logits - top), axis=0, keepdims=True)
    each(1, n, lambda k: stat_copy(k).start())
    stats[me] = own_stats[...]

    def settle(k):
        row_copy(k).wait_send()
        meta_copy(k).wait_send()
        back_copy(k).wait()

    each(1, groups, settle)
    own_back.wait()
    each(1, half, lambda k: fin_copy(k).wait_send())
    each(0, half, lambda k: pass_on(k).wait_send())
    each(1, n, lambda k: stat_copy(k).wait())
    tops = stats[:, 0, :]
    best = jnp.max(tops, axis=0, keepdims=True)
    total = jnp.sum(stats[:, 1, :] * jnp.exp(tops - best), axis=0, keepdims=True)
    lse_ref[...] = best + jnp.log(total)


def local(
    residual,
    lengths,
    adapter_ids,
    ffn_gain,
    w_gate_up,
    w_down,
    adapter_input_first,
    ad_out_b,
    ad_down_a,
    adapter_down_second,
    final_gain,
    head_weight,
):
    n_req, seq, width = residual.shape
    groups = lax.axis_size("ad")
    n_q = lax.axis_size("req")
    n = n_q * groups
    per_dev = adapter_input_first.shape[0]
    rank = ad_down_a.shape[1]
    units = w_down.shape[0]
    shard = head_weight.shape[1]
    total_req = n * n_req
    rows = groups // CHUNKS * seq
    f32 = jnp.float32
    bf16 = jnp.bfloat16
    ina = adapter_input_first.reshape(per_dev * 2 * rank, width)
    outb = ad_out_b.reshape(per_dev * 2 * rank, units)
    downa = ad_down_a.reshape(per_dev * rank, units)
    downb = adapter_down_second.reshape(per_dev * rank, width)
    head_t = head_weight.T
    dma = pltpu.SemaphoreType.DMA
    vm = pltpu.VMEM
    back, logits_t, lse = pl.pallas_call(
        functools.partial(layer_kernel, n_q, groups, per_dev, n_req),
        out_shape=(
            jax.ShapeDtypeStruct((groups, seq, width), bf16),
            jax.ShapeDtypeStruct((shard, total_req), f32),
            jax.ShapeDtypeStruct((1, total_req), f32),
        ),
        in_specs=[ANY_SPEC] * 3 + [VMEM_SPEC] * 2 + [ANY_SPEC] * 7,
        out_specs=(VMEM_SPEC,) * 3,
        scratch_shapes=[
            pltpu.SMEM((n_req,), jnp.int32),
            pltpu.SMEM((n_req,), jnp.int32),
            vm((n_req, seq, width), bf16),
            vm((groups, seq, width), bf16),
            vm((groups, 8, 128), jnp.int32),
            vm((groups, seq, width), bf16),
            vm((groups, 8, 128), jnp.int32),
            vm((rows, width), bf16),
            vm((rows, per_dev * 2 * rank), bf16),
            vm((rows, per_dev * 2 * rank), bf16),
            vm((rows, units), bf16),
            vm((rows, width), f32),
            vm((groups, seq, width), bf16),
            vm((groups, width + 128), f32),
            vm(w_gate_up.shape, bf16),
            vm(w_down.shape, bf16),
            vm(ina.shape, bf16),
            vm(outb.shape, bf16),
            vm(downa.shape, bf16),
            vm(downb.shape, bf16),
            vm(head_t.shape, bf16),
            vm((groups, width + 128), bf16),
            vm((n, groups, width + 128), bf16),
            vm((n * groups, width + 128), f32),
            vm((n, 2, total_req), f32),
            vm((2, total_req), f32),
            dma((3,)), dma((15,)), dma(()),
            dma((groups,)), dma((groups,)), dma((groups,)), dma((groups,)),
            dma((groups,)), dma((groups,)),
            dma((n // 2,)), dma((n // 2,)), dma((n // 2,)), dma((n // 2,)),
            dma((n,)), dma((n,)),
        ],
        compiler_params=pltpu.CompilerParams(
            collective_id=0, has_side_effects=True, vmem_limit_bytes=60 << 20
        ),
    )(
        adapter_ids, lengths, residual, ffn_gain, final_gain, w_gate_up, w_down,
        ina, outb, downa, downb, head_t,
    )
    holder = adapter_ids // per_dev
    place = (holder[:, None] == jnp.arange(groups, dtype=jnp.int32)[None, :]).astype(bf16)
    layer_out = jnp.einsum("rh,hsf->rsf", place, back, preferred_element_type=f32).astype(bf16)
    return layer_out, (logits_t - lse).T


def solution(mesh):
    in_specs = (
        P(("req", "ad"), None, None),
        P(("req", "ad")),
        P(("req", "ad")),
        P(),
        P(),
        P(),
        P("ad", None, None),
        P("ad", None, None, None),
        P("ad", None, None),
        P("ad", None, None),
        P(),
        P(None, ("req", "ad")),
    )
    out_specs = (P(("req", "ad"), None, None), P(None, ("req", "ad")))
    return jax.shard_map(local, mesh=mesh, in_specs=in_specs, out_specs=out_specs, check_vma=False)
```

time: 356 us -> 64.7 us (0.18)
  blocking collectives: 222 us -> 0 us
  waiting for transfers between devices: 68.2 us -> 0 us
  Pallas kernels: 0 us -> 58.6 us
  matrix products: 29 us -> 1.43 us
  starting transfers between devices: 19.7 us -> 0 us
  local copies, waits for them, and re-layouts: 9.53 us -> 0.88 us
    all_to_all x1 -> x0, blocking collectives: 74.3 us -> none  [local(): lax.all_to_all(delta, 'ad', split_axis=0, concat_axis=0, tiled=True)]
    all_gather x1 -> x0, blocking collectives: 69.7 us -> none  [local(): lax.all_gather(final, ('req', 'ad'), axis=0, tiled=True)]
    all_to_all x4 -> x0, waiting for transfers between devices: 68.2 us -> none  [the longest x1 35.1 us: local(): lax.all_to_all(place(hidden_kept), 'ad', split_axis=0, concat_axis=0, til...]
    pallas_call x0 -> x1, Pallas kernels: none -> 58.6 us  [local(): pl.pallas_call(functools.partial(layer_kernel, n_q, groups, per_dev, n_re...]
    psum x1 -> x0, blocking collectives: 41.3 us -> none  [local(): lax.psum(jnp.sum(jnp.exp(logits - highest[:, None]), axis=1), ('req', 'ad'))]
    pmax x1 -> x0, blocking collectives: 36.9 us -> none  [local(): highest = lax.pmax(local_max, ('req', 'ad'))]
    dot_general x12 -> x1, matrix products: 29 us -> 1.43 us  [local(): jnp.einsum('rh,hsf->rsf', place, back, preferred_element_type=f32)]
    all_to_all x4 -> x0, starting transfers between devices: 19.7 us -> none  [the longest x1 7.25 us: local(): lax.all_to_all(slot_rows, 'ad', split_axis=0, concat_axis=0, tiled=True)]
  transfers between devices with their start and end apart: 4 -> 0, of which waited for: 4 -> 0; matrix products, arithmetic and copies ran while one was open for 2% -> 0% of each run, Pallas kernels for 0% -> 0%
where the time goes in v2:
time: 64.7 us; the launch traced here: 64.4 us
  Pallas kernels  58.6 us (91%)
  other arithmetic  2.91 us (4%)
  matrix products  1.43 us (2%)
  local copies, waits for them, and re-layouts  0.88 us (1%)
  between operations  0.65 us (1%)
    pallas_call x1, Pallas kernels, local(): pl.pallas_call(functools.partial(layer_kernel, n_q, groups, per_dev, n_re...  58.6 us
    transpose x1, other arithmetic, local(): return (layer_out, (logits_t - lse).T)  2.24 us
    dot_general x1, matrix products, local(): jnp.einsum('rh,hsf->rsf', place, back, preferred_element_type=f32)  1.43 us

profile of v2, /device:TPU:0, one launch (start us, length us, event | category | flops | bytes accessed | tf_op | source)
XLA Modules:
  0.0 64.4 jit_solution(14225875726186458254)
XLA Ops:
  0.6 0.7 %and_select_fusion = s32[8]{0:T(128)S(1)} fusion(s32[8]{0:T(128)} %ids_hbm.1), kind=kLoop, calls=%fused_computation.6 | loop fusion | flops 120 | bytes 64 | tf_op jit(solution)/shard_map/jit(floor_divide)/jit(_where)/select_n | solution.py:400
  1.3 58.6 %shard_map.131 = (bf16[8,32,1152]{2,1,0:T(8,128)(2,1)}, f32[1000,256]{1,0:T(8,128)}, f32[1,256]{1,0:T(1,128)}) custom-call(s32[8]{0:T(128)} %ids_hbm.1, s32[8]{0:T(128)} %len_hbm.1, bf16[8,32,1152]{2,1,0:T(8,128)(2,1)} %x_hbm.1, f32[1152]{0:T(1024)} %gain_ref.1, f32[1152]{0:T(1024)} %fgain_ref.1, bf16[2,1152,3072]{2,1,0:T(8,128)(2,1)} %wgu_hbm.1, ...), custom_call_target="tpu_custom_call" | custom-call | tf_op jit(solution)/shard_map/pallas_call | solution.py:351
  59.9 1.4 %convolution_convert_fusion = bf16[8,32,1152]{2,0,1:T(8,128)(2,1)S(1)} fusion(bf16[8,32,1152]{2,1,0:T(8,128)(2,1)} %get-tuple-element.5, s32[8]{0:T(128)S(1)} %and_select_fusion), kind=kOutput, calls=%fused_computation | convolution fusion | flops 5013568 | bytes 1179680 | tf_op jit(solution)/shard_map/rh,hsf->rsf/dot_general | solution.py:402
  61.3 0.9 %copy.15 = bf16[8,32,1152]{2,1,0:T(8,128)(2,1)} copy(bf16[8,32,1152]{2,0,1:T(8,128)(2,1)S(1)} %convolution_convert_fusion) | data formatting | bytes 1179648
  62.2 2.2 %subtract_bitcast_fusion = f32[256,1000]{0,1:T(8,128)} fusion(f32[1000,256]{1,0:T(8,128)} %get-tuple-element.6, f32[256]{0:T(256)} %bitcast.16), kind=kLoop, calls=%fused_computation.1 | loop fusion | flops 256000 | bytes 2049024 | tf_op jit(solution)/shard_map/transpose | solution.py:403

commit v3 on v2

--- a/solution.py
+++ b/solution.py
@@ -8,7 +8,7 @@
 from jax.sharding import PartitionSpec as P
 
 epsilon = 1e-05
-CHUNKS = 1
+CHUNKS = 2
 MESH = pl.DeviceIdType.MESH
 VMEM_SPEC = pl.BlockSpec(memory_space=pltpu.VMEM)
 ANY_SPEC = pl.BlockSpec(memory_space=pl.ANY)
@@ -19,7 +19,8 @@
     n_q, groups, per_dev, n_req,
     ids_hbm, len_hbm, x_hbm, gain_ref, fgain_ref, wgu_hbm, wd_hbm, ina_hbm, outb_hbm,
     downa_hbm, downb_hbm, wh_hbm,
-    back, lt_ref, lse_ref,
+    out_ref, lt_ref, lse_ref,
+    back,
     ids, lens, xs, stage, mstage, recv, mrecv, normed, low_g, low_u, hidden, mixed, y, last,
     wgu, wd, ina, outb, downa, downb, wh,
     fin, gathered, wide, stats, own_stats,
@@ -306,6 +307,8 @@
 
     each(1, groups, settle)
     own_back.wait()
+    for r in range(n_req):
+        out_ref[r] = back[lax.div(ids[r], per_dev)]
     each(1, half, lambda k: fin_copy(k).wait_send())
     each(0, half, lambda k: pass_on(k).wait_send())
     each(1, n, lambda k: stat_copy(k).wait())
@@ -348,16 +351,17 @@
     head_t = head_weight.T
     dma = pltpu.SemaphoreType.DMA
     vm = pltpu.VMEM
-    back, logits_t, lse = pl.pallas_call(
+    layer_out, logits_t, lse = pl.pallas_call(
         functools.partial(layer_kernel, n_q, groups, per_dev, n_req),
         out_shape=(
-            jax.ShapeDtypeStruct((groups, seq, width), bf16),
+            jax.ShapeDtypeStruct((n_req, seq, width), bf16),
             jax.ShapeDtypeStruct((shard, total_req), f32),
             jax.ShapeDtypeStruct((1, total_req), f32),
         ),
         in_specs=[ANY_SPEC] * 3 + [VMEM_SPEC] * 2 + [ANY_SPEC] * 7,
         out_specs=(VMEM_SPEC,) * 3,
         scratch_shapes=[
+            vm((groups, seq, width), bf16),
             pltpu.SMEM((n_req,), jnp.int32),
             pltpu.SMEM((n_req,), jnp.int32),
             vm((n_req, seq, width), bf16),
@@ -397,9 +401,6 @@
         adapter_ids, lengths, residual, ffn_gain, final_gain, w_gate_up, w_down,
         ina, outb, downa, downb, head_t,
     )
-    holder = adapter_ids // per_dev
-    place = (holder[:, None] == jnp.arange(groups, dtype=jnp.int32)[None, :]).astype(bf16)
-    layer_out = jnp.einsum("rh,hsf->rsf", place, back, preferred_element_type=f32).astype(bf16)
     return layer_out, (logits_t - lse).T
 
 

time: 64.7 us -> 57.5 us (0.89)
  Pallas kernels: 58.6 us -> 52.4 us
  matrix products: 1.43 us -> 0 us
  local copies, waits for them, and re-layouts: 0.88 us -> 1.92 us
  other arithmetic: 2.91 us -> 2.25 us
    pallas_call x1, Pallas kernels: 58.6 us -> 52.4 us  [local(): pl.pallas_call(functools.partial(layer_kernel, n_q, groups, per_dev, n_re...]
    dot_general x1 -> x0, matrix products: 1.43 us -> none  [local(): jnp.einsum('rh,hsf->rsf', place, back, preferred_element_type=f32)]
    unnamed x1, local copies, waits for them, and re-layouts: 0.88 us -> 1.92 us
    select_n x1 -> x0, other arithmetic: 0.67 us -> none  [local(): holder = adapter_ids // per_dev]
where the time goes in v3:
time: 57.5 us; the launch traced here: 57.2 us
  Pallas kernels  52.4 us (91%)
  other arithmetic  2.25 us (4%)
  local copies, waits for them, and re-layouts  1.92 us (3%)
  between operations  0.64 us (1%)
    pallas_call x1, Pallas kernels, local(): pl.pallas_call(functools.partial(layer_kernel, n_q, groups, per_dev, n_re...  52.4 us
    transpose x1, other arithmetic, local(): return (layer_out, (logits_t - lse).T)  2.25 us
    unnamed x1, local copies, waits for them, and re-layouts  1.92 us

profile of v3, /device:TPU:0, one launch (start us, length us, event | category | flops | bytes accessed | tf_op | source)
XLA Modules:
  0.0 57.2 jit_solution(4336424293994269682)
XLA Ops:
  0.6 52.4 %shard_map.131 = (bf16[8,32,1152]{2,1,0:T(8,128)(2,1)}, f32[1000,256]{1,0:T(8,128)}, f32[1,256]{1,0:T(1,128)}) custom-call(s32[8]{0:T(128)} %ids_hbm.1, s32[8]{0:T(128)} %len_hbm.1, bf16[8,32,1152]{2,1,0:T(8,128)(2,1)} %x_hbm.1, f32[1152]{0:T(1024)} %gain_ref.1, f32[1152]{0:T(1024)} %fgain_ref.1, bf16[2,1152,3072]{2,1,0:T(8,128)(2,1)} %wgu_hbm.1, ...), custom_call_target="tpu_custom_call" | custom-call | tf_op jit(solution)/shard_map/pallas_call | solution.py:354
  53.1 2.2 %subtract_bitcast_fusion = f32[256,1000]{0,1:T(8,128)} fusion(f32[1000,256]{1,0:T(8,128)} %get-tuple-element.6, f32[256]{0:T(256)} %bitcast.13), kind=kLoop, calls=%fused_computation | loop fusion | flops 256000 | bytes 2049024 | tf_op jit(solution)/shard_map/transpose | solution.py:404
  55.3 1.9 %copy.15 = bf16[8,32,1152]{2,1,0:T(8,128)(2,1)} copy(bf16[8,32,1152]{2,1,0:T(8,128)(2,1)} %get-tuple-element.10) | data formatting | bytes 1179648
